TPU v7x, 32 devices: a whole 2x2x4 slice. The times are simulated.
32 devices in a mesh: groups: 2 (over y), row: 8 (over z, x), col: 2 (over core).
Axes of the slice: x: 2, y: 2, z: 4, core: 2. Of those that a mesh axis runs over, the one named last changes fastest.
Arguments:
- concentration: float32 [512, 256, 256], P('groups', 'row', 'col'), parts along dimension 0, may hold values from -6 to 6
- species: int32 [2], P('groups'), parts along dimension 0, may hold values from 0 to 63
- reaction_rates: float32 [64], replicated, may hold values from 0.2 to 0.8
- levels: float32 [64], replicated, may hold values from -1 to 1
- sweep_flags: int32 [2, 3], replicated, may hold values from 0 to 1
- explicit_line: float32 [256, 256], replicated, may hold values from -0.5 to 1.2
- inverse_line: float32 [256, 256], replicated, may hold values from -0.5 to 1.2
- explicit_depth: float32 [256, 256], replicated, may hold values from -0.5 to 1.2
- inverse_depth: float32 [256, 256], replicated, may hold values from -0.5 to 1.2
Outputs:
- advanced: float32 [512, 256, 256], P('groups', 'row', 'col'), parts along dimension 0
There are 2 independent parts, one for each index of `groups`. A program takes and returns all parts, laid end to end along the dimension named above; an argument that names none is the same for every part. Nothing has to cross between parts.
All inputs are finite; a program needn't handle non-finite values.
Results may differ from a plain program's by a relative error of at most 0.00011.
Values sent between devices are 32-bit elements; how exact they have to be, the bound alone decides.
A program may use at most 64 MiB of HBM per device.

v0:
```python
import functools

import jax
import jax.numpy as jnp
from jax import lax
from jax.experimental import pallas as pl
from jax.experimental.pallas import tpu as pltpu
from jax.sharding import PartitionSpec as P

MESH = pl.DeviceIdType.MESH
LANES = 128


def react(v, rate, level):
    return v - rate * jnp.tanh(v - level)


def split(v):
    hi = v.astype(jnp.bfloat16)
    lo = (v - hi.astype(jnp.float32)).astype(jnp.bfloat16)
    return hi, lo


def dot3(a, b):
    (ah, al), (bh, bl) = a, b
    dot = functools.partial(jnp.dot, preferred_element_type=jnp.float32)
    return dot(ah, bh) + (dot(ah, bl) + dot(al, bh))


def load_columns(ref, r, width):
    lines, rows, lanes = ref.shape
    if rows % 8 == 0:
        flat = ref.reshape(lines * rows, lanes)
        parts = [flat[pl.ds(r + i, lines, stride=rows), :] for i in range(width)]
    else:
        parts = [ref[:, r + i, :] for i in range(width)]
    return jnp.concatenate(parts, axis=1)


def store_columns(ref, r, width, value):
    lines, rows, lanes = ref.shape
    for i in range(width):
        part = value[:, i * lanes : (i + 1) * lanes]
        if rows % 8 == 0:
            flat = ref.reshape(lines * rows, lanes)
            flat[pl.ds(r + i, lines, stride=rows), :] = part
        else:
            ref[:, r + i, :] = part


def middle_kernel(
    n, L, R, C, G,
    scal_ref, mats_ref, x_hbm, f_hbm,
    x, y, z, w, v, h, t, u, mh, ml,
    x_sem, own1, own2, send1, recv1, send2, recv2, a_send, a_recv, b_send, b_recv,
):
    me = lax.axis_index("row")
    q = lax.axis_index("col")
    rate, level = scal_ref[0], scal_ref[1]
    per = L // C
    pair = 2 if per % 2 == 0 else 1
    group = R // G

    for g in range(G):
        rows = pl.ds(g * group, group)
        pltpu.make_async_copy(x_hbm.at[:, rows], x.at[:, rows], x_sem.at[g]).start()

    barrier = pltpu.get_barrier_semaphore()

    def greet(j, carry):
        pl.semaphore_signal(
            barrier, inc=1, device_id={"row": lax.rem(me + j, n)}, device_id_type=MESH
        )
        return carry

    lax.fori_loop(1, n, greet, 0)
    pl.semaphore_signal(barrier, inc=1, device_id={"col": 1 - q}, device_id_type=MESH)

    for m in range(mats_ref.shape[0]):
        hi, lo = split(mats_ref[m])
        mh[m] = hi
        ml[m] = lo

    first = (mh[0], ml[0])
    cols = 2 if group % 2 == 0 else 1
    for g in range(G):
        rows = pl.ds(g * group, group)
        pltpu.make_async_copy(x_hbm.at[:, rows], x.at[:, rows], x_sem.at[g]).wait()

        def sweep(s, carry, g=g):
            r = g * group + s * cols
            k = split(react(load_columns(x, r, cols), rate, level))
            store_columns(y, r, cols, dot3(first, k))
            return carry

        if R % 8 == 0:
            lax.fori_loop(0, group // cols, sweep, 0)
        else:
            for s in range(group // cols):
                sweep(s, 0)

    pl.semaphore_wait(barrier, n)

    def send_chunk(c, carry):
        def send_to(j, inner):
            d = lax.rem(me + j, n)
            pltpu.make_async_remote_copy(
                src_ref=y.at[pl.ds(d * L + c * per, per)],
                dst_ref=z.at[pl.ds(c * per, per), me],
                send_sem=send1,
                recv_sem=recv1.at[c],
                device_id={"row": d},
                device_id_type=MESH,
            ).start()
            return inner

        lax.fori_loop(1, n, send_to, 0)
        pltpu.make_async_copy(
            y.at[pl.ds(me * L + c * per, per)], z.at[pl.ds(c * per, per), me], own1.at[c]
        ).start()
        return carry

    lax.fori_loop(0, C, send_chunk, 0)

    half = n * R // 2
    mine = pl.ds(pl.multiple_of(q * half, half), half)
    theirs = pl.ds(pl.multiple_of((1 - q) * half, half), half)
    lanes_mine = pl.ds(pl.multiple_of(q * LANES, LANES), LANES)
    lanes_theirs = pl.ds(pl.multiple_of((1 - q) * LANES, LANES), LANES)
    peer = {"col": 1 - q}

    def chunk(c, carry):
        at = pl.ds(c * per, per)
        pltpu.make_async_copy(z.at[at, pl.ds(0, n - 1)], z.at[at, pl.ds(0, n - 1)], recv1.at[c]).wait()
        pltpu.make_async_copy(
            y.at[pl.ds(me * L + c * per, per)], z.at[at, me], own1.at[c]
        ).wait()

        line = tuple(jnp.concatenate([m[1, mine, :], m[1, theirs, :]], axis=0) for m in (mh, ml))
        for s in range(0, per, pair):
            i = c * per + s
            k = jnp.concatenate([z[i + e].reshape(n * R, LANES) for e in range(pair)], axis=1)
            out = dot3(line, split(react(k, rate, level)))
            for e in range(pair):
                part = out[:, e * LANES : (e + 1) * LANES]
                v[i + e, :, lanes_mine] = part[:half]
                w[i + e] = part[half:]
        to_peer = pltpu.make_async_remote_copy(
            src_ref=w.at[at],
            dst_ref=v.at[at, :, lanes_mine],
            send_sem=a_send.at[c],
            recv_sem=a_recv.at[c],
            device_id=peer,
            device_id_type=MESH,
        )
        to_peer.start()
        to_peer.wait()

        k = v[at].reshape(per * half, 2 * LANES)
        k = dot3(split(react(k, rate, level)), (mh[2], ml[2]))
        depth = tuple(
            jnp.concatenate([m[3, :, lanes_mine], m[3, :, lanes_theirs]], axis=1) for m in (mh, ml)
        )
        k = dot3(split(react(k, rate, level)), depth)
        t[at, mine, :] = k[:, :LANES].reshape(per, half, LANES)
        h[at] = k[:, LANES:].reshape(per, half, LANES)
        to_peer = pltpu.make_async_remote_copy(
            src_ref=h.at[at],
            dst_ref=t.at[at, mine, :],
            send_sem=b_send.at[c],
            recv_sem=b_recv.at[c],
            device_id=peer,
            device_id_type=MESH,
        )
        to_peer.start()
        to_peer.wait()

        line = (mh[4], ml[4])
        for s in range(0, per, pair):
            i = c * per + s
            k = jnp.concatenate([t[i + e] for e in range(pair)], axis=1)
            out = dot3(line, split(react(k, rate, level)))
            for e in range(pair):
                u[i + e] = out[:, e * LANES : (e + 1) * LANES].reshape(n, R, LANES)

        def send_to(j, inner):
            d = lax.rem(me + j, n)
            pltpu.make_async_remote_copy(
                src_ref=u.at[at, d],
                dst_ref=f_hbm.at[pl.ds(me * L + c * per, per)],
                send_sem=send2,
                recv_sem=recv2,
                device_id={"row": d},
                device_id_type=MESH,
            ).start()
            return inner

        lax.fori_loop(1, n, send_to, 0)
        pltpu.make_async_copy(
            u.at[at, me], f_hbm.at[pl.ds(me * L + c * per, per)], own2
        ).start()
        return carry

    lax.fori_loop(0, C, chunk, 0)

    away = y.at[pl.ds(0, (n - 1) * L)]
    pltpu.make_async_copy(away, away, send1).wait()
    pltpu.make_async_copy(away, away, send2).wait()
    own = y.at[pl.ds(0, L)]
    pltpu.make_async_copy(own, own, own2).wait()
    pltpu.make_async_copy(away, away, recv2).wait()


def last_kernel(scal_ref, mat_ref, f_ref, o_ref):
    rate, level = scal_ref[0], scal_ref[1]
    R = f_ref.shape[1]
    matrix = split(mat_ref[...])
    cols = 2 if R % 2 == 0 else 1

    def sweep(s, carry):
        k = split(react(load_columns(f_ref, s * cols, cols), rate, level))
        store_columns(o_ref, s * cols, cols, dot3(matrix, k))
        return carry

    if R % 8 == 0:
        lax.fori_loop(0, R // cols, sweep, 0)
    else:
        for s in range(R // cols):
            sweep(s, 0)


def on_device(
    n,
    concentration,
    species,
    reaction_rates,
    levels,
    sweep_flags,
    explicit_line,
    inverse_line,
    explicit_depth,
    inverse_depth,
):
    picker = (jnp.arange(reaction_rates.shape[0], dtype=jnp.int32) == species[0]).astype(
        jnp.float32
    )
    scalars = jnp.stack([jnp.sum(reaction_rates * picker), jnp.sum(levels * picker)])
    line = jnp.dot(inverse_line, explicit_line, precision=lax.Precision.HIGHEST)
    depth = jnp.dot(
        explicit_depth.T, inverse_depth.T, precision=lax.Precision.HIGHEST
    )
    order = [(0, 0), (0, 1), (0, 2), (1, 2), (1, 1), (1, 0)]
    stack = jnp.stack([depth if d == 2 else line for _, d in order])
    flags = jnp.stack([sweep_flags[s, d] for s, d in order])
    mats = jnp.where(flags[:, None, None] == 1, stack[:, ::-1, ::-1], stack)

    lines, R, lanes = concentration.shape
    L = lines // n
    C = max(1, L // 4)
    G = max(1, R // 8)
    f32 = jnp.float32
    any_spec = pl.BlockSpec(memory_space=pl.ANY)
    smem = pl.BlockSpec(memory_space=pltpu.SMEM)
    dma = pltpu.SemaphoreType.DMA
    half = n * R // 2
    field = pl.pallas_call(
        functools.partial(middle_kernel, n, L, R, C, G),
        out_shape=jax.ShapeDtypeStruct(concentration.shape, f32),
        in_specs=[smem, pl.BlockSpec(memory_space=pltpu.VMEM), any_spec],
        out_specs=any_spec,
        scratch_shapes=[
            pltpu.VMEM((lines, R, lanes), f32),
            pltpu.VMEM((lines, R, lanes), f32),
            pltpu.VMEM((L, n, R, lanes), f32),
            pltpu.VMEM((L, half, lanes), f32),
            pltpu.VMEM((L, half, 2 * lanes), f32),
            pltpu.VMEM((L, half, lanes), f32),
            pltpu.VMEM((L, 2 * half, lanes), f32),
            pltpu.VMEM((L, n, R, lanes), f32),
            pltpu.VMEM(mats.shape, jnp.bfloat16),
            pltpu.VMEM(mats.shape, jnp.bfloat16),
            dma((G,)),
            dma((C,)),
            dma,
            dma,
            dma((C,)),
            dma,
            dma,
            dma((C,)),
            dma((C,)),
            dma((C,)),
            dma((C,)),
        ],
        compiler_params=pltpu.CompilerParams(
            collective_id=0, has_side_effects=True, vmem_limit_bytes=56 << 20
        ),
    )(scalars, mats, concentration)

    rows = R // G
    return pl.pallas_call(
        last_kernel,
        grid=(G,),
        out_shape=jax.ShapeDtypeStruct(concentration.shape, f32),
        in_specs=[
            smem,
            pl.BlockSpec((lines, lines), lambda g: (0, 0)),
            pl.BlockSpec((lines, rows, lanes), lambda g: (0, g, 0)),
        ],
        out_specs=pl.BlockSpec((lines, rows, lanes), lambda g: (0, g, 0)),
        compiler_params=pltpu.CompilerParams(vmem_limit_bytes=32 << 20),
    )(scalars, mats[5], field)


def solution(mesh):
    in_specs = (P("groups", "row", "col"), P("groups"), P(), P(), P(), P(), P(), P(), P())
    out_specs = P("groups", "row", "col")
    return jax.shard_map(
        functools.partial(on_device, mesh.shape["row"]),
        mesh=mesh, in_specs=in_specs, out_specs=out_specs, check_vma=False,
    )
```

profile of v0, /device:TPU:10, one launch (start us, length us, event | category | flops | bytes accessed | tf_op | source)
XLA Modules:
  0.0 218.1 jit_solution(5356534052101593642)
XLA Ops:
  0.0 0.0 copy-start
  0.0 0.0 copy-start.5
  0.0 0.0 copy-start.4
  0.7 1.3 fusion
  2.0 1.8 pad_maximum_fusion.scal_ref
  3.8 1.6 fusion.2
  5.4 3.8 %stack.46 = s32[6]{0:T(128)S(1)} concatenate(s32[1]{0:T(128)} %bitcast.3, s32[1]{0:T(128)} %bitcast.4, s32[1]{0:T(128)} %bitcast.5, s32[1]{0:T(128)} %bitcast.6, s32[1]{0:T(128)} %bitcast.7, s32[1]{0:T(128)} %bitcast.8), dimensions={0} | concatenate | bytes 48 | tf_op jit(solution)/shard_map/stack | solution.py:254
  9.3 0.0 copy-done
  9.3 1.3 constant_dynamic-update-slice_fusion.5
  10.6 0.0 copy-done.5
  10.6 0.0 copy-done.4
  10.6 0.6 constant_dynamic-update-slice_fusion.3
  11.3 2.1 rev.3
  13.5 0.3 broadcast_select_fusion.mats_ref
  13.7 0.0 copy-start.3
  13.8 1.1 copy-done.3
  14.9 0.0 copy-start.2
  14.9 193.8 %shard_map.91.f_ref = f32[256,32,128]{2,1,0:T(8,128)} custom-call(f32[2]{0:T(128)} %pad_maximum_fusion.scal_ref, f32[6,256,256]{2,1,0:T(8,128)} %copy-done.3, f32[256,32,128]{2,1,0:T(8,128)} %x_hbm.1), custom_call_target="tpu_custom_call" | custom-call | tf_op jit(solution)/shard_map/pallas_call | solution.py:266
  208.7 0.0 copy-done.2
  208.7 0.0 copy-start.1
  208.7 2.2 copy-done.1
  210.9 7.2 %shard_map.92 = f32[256,32,128]{2,1,0:T(8,128)} custom-call(f32[2]{0:T(128)S(1)} %copy-done.2, f32[256,256]{1,0:T(8,128)S(1)} %slice_bitcast_fusion.mat_ref, f32[256,32,128]{2,1,0:T(8,128)S(1)} %copy-done.1), custom_call_target="tpu_custom_call" | custom-call | tf_op jit(solution)/shard_map/pallas_call | solution.py:300
  (6 shorter events, 0.1 us)
Async XLA Ops:
  0.0 9.3 %copy-start = (f32[256,256]{1,0:T(8,128)S(1)}, f32[256,256]{1,0:T(8,128)}, u32[]{:S(2)}) copy-start(f32[256,256]{1,0:T(8,128)} %param.15) | copy-start | bytes 786436
  0.0 10.6 %copy-start.5 = (f32[256,256]{1,0:T(8,128)S(1)}, f32[256,256]{1,0:T(8,128)}, u32[]{:S(2)}) copy-start(f32[256,256]{1,0:T(8,128)} %param.17) | copy-start | bytes 786436
  0.0 10.6 %copy-start.4 = (f32[256,256]{1,0:T(8,128)S(1)}, f32[256,256]{1,0:T(8,128)}, u32[]{:S(2)}) copy-start(f32[256,256]{1,0:T(8,128)} %param.16) | copy-start | bytes 786436
  13.7 1.1 copy-start.3
  14.9 193.8 %copy-start.2 = (f32[2]{0:T(128)S(1)}, f32[2]{0:T(128)}, u32[]{:S(2)}) copy-start(f32[2]{0:T(128)} %pad_maximum_fusion.scal_ref) | copy-start | bytes 28
  208.7 2.2 %copy-start.1 = (f32[256,32,128]{2,1,0:T(8,128)S(1)}, f32[256,32,128]{2,1,0:T(8,128)}, u32[]{:S(2)}) copy-start(f32[256,32,128]{2,1,0:T(8,128)} %shard_map.91.f_ref) | copy-start | bytes 12582916
where the time goes:
time: 219 us; the launch traced here: 218 us
  Pallas kernels  201 us (92%)
  local copies, waits for them, and re-layouts  10.9 us (5%)
  other arithmetic  3.39 us (2%)
    pallas_call x1, Pallas kernels, on_device(): pl.pallas_call(functools.partial(middle_kernel, n, L, R, C, G), out_shape...  194 us
    pallas_call x1, Pallas kernels, on_device(): pl.pallas_call(last_kernel, grid=(G,), out_shape=jax.ShapeDtypeStruct(con...  7.21 us

commit v1 on v0

v1 whole, which is shorter than its diff:
```python
import functools

import jax
import jax.numpy as jnp
import numpy as np
from jax import lax
from jax.experimental import pallas as pl
from jax.experimental.pallas import tpu as pltpu
from jax.sharding import PartitionSpec as P

MESH = pl.DeviceIdType.MESH
LANES = 128


def react(v, rate, level):
    return v - rate * jnp.tanh(v - level)


def split(v):
    hi = v.astype(jnp.bfloat16)
    lo = (v - hi.astype(jnp.float32)).astype(jnp.bfloat16)
    return hi, lo


def dot3(a, b):
    (ah, al), (bh, bl) = a, b
    dot = functools.partial(jnp.dot, preferred_element_type=jnp.float32)
    return dot(ah, bh) + (dot(ah, bl) + dot(al, bh))


def load_columns(ref, r, width, start, lines):
    rows, lanes = ref.shape[1:]
    if rows % 8 == 0:
        flat = ref.reshape(ref.shape[0] * rows, lanes)
        parts = [flat[pl.ds(start * rows + r + i, lines, stride=rows), :] for i in range(width)]
    else:
        parts = [ref[start : start + lines, r + i, :] for i in range(width)]
    return jnp.concatenate(parts, axis=1)


def store_columns(ref, r, width, value):
    lines, rows, lanes = ref.shape
    for i in range(width):
        part = value[:, i * lanes : (i + 1) * lanes]
        if rows % 8 == 0:
            flat = ref.reshape(lines * rows, lanes)
            flat[pl.ds(r + i, lines, stride=rows), :] = part
        else:
            ref[:, r + i, :] = part


def move(source, target):
    return jnp.dot(source, target, preferred_element_type=jnp.float32).astype(jnp.bfloat16)


def orientations(matrix):
    size = matrix.shape[0]
    i = lax.broadcasted_iota(jnp.int32, (size, size), 0)
    j = lax.broadcasted_iota(jnp.int32, (size, size), 1)
    exchange = jnp.where(i + j == size - 1, 1.0, 0.0).astype(jnp.bfloat16)
    halves = split(matrix)
    return halves, tuple(move(move(exchange, m), exchange) for m in halves)


def choose(flag, plain, turned):
    where = jnp.full(plain[0].shape, flag, jnp.int32) == 1
    return tuple(
        jnp.where(where, b.astype(jnp.float32), a.astype(jnp.float32)).astype(jnp.bfloat16)
        for a, b in zip(plain, turned)
    )


def fold(inverse, explicit, transposed):
    if transposed:
        inverse, explicit = explicit.T, inverse.T
    return jnp.dot(
        inverse,
        explicit,
        precision=lax.Precision.HIGHEST,
        preferred_element_type=jnp.float32,
    )


def loop_columns(count, ref, body):
    if ref.shape[1] % 8 == 0:
        lax.fori_loop(0, count, body, 0)
    else:
        for s in range(count):
            body(s, 0)


def kernel(
    n, L, R, C, G,
    species, rates, levels, flags, e_line, p_line, e_depth, p_depth, pick_a, pick_b,
    x_hbm, o_hbm,
    x, y, z, w, v, h, t, u, f, mh, ml, ma, mb,
    x_sem, own1, own2, send1, recv1, send2, recv2, a_send, a_recv, b_send, b_recv, o_sem,
):
    me = lax.axis_index("row")
    q = lax.axis_index("col")
    per = L // C
    pair = 2 if per % 2 == 0 else 1
    group = R // G

    for g in range(G):
        rows = pl.ds(g * group, group)
        pltpu.make_async_copy(x_hbm.at[:, rows], x.at[:, rows], x_sem.at[g]).start()

    barrier = pltpu.get_barrier_semaphore()

    def greet(j, carry):
        pl.semaphore_signal(
            barrier, inc=1, device_id={"row": lax.rem(me + j, n)}, device_id_type=MESH
        )
        return carry

    lax.fori_loop(1, n, greet, 0)
    pl.semaphore_signal(barrier, inc=1, device_id={"col": 1 - q}, device_id_type=MESH)

    kind = species[0]
    rate, level = rates[kind], levels[kind]

    def keep(slot, flag, plain, turned):
        mh[slot], ml[slot] = choose(flag, plain, turned)

    lines = orientations(fold(p_line[...], e_line[...], False))
    keep(0, flags[0, 0], *lines)
    keep(1, flags[0, 1], *lines)
    keep(4, flags[1, 1], *lines)
    final = choose(flags[1, 0], *lines)
    if C > 1:
        ma[...] = (
            jnp.dot(final[0], pick_a[0], preferred_element_type=jnp.float32)
            + jnp.dot(final[1], pick_a[1], preferred_element_type=jnp.float32)
        ).astype(jnp.bfloat16)
    mb[...] = (
        jnp.dot(final[0], pick_b[0], preferred_element_type=jnp.float32)
        + jnp.dot(final[1], pick_b[1], preferred_element_type=jnp.float32)
    ).astype(jnp.bfloat16)

    def send_rows(c, rows):
        def send_to(j, inner):
            d = lax.rem(me + j, n)
            pltpu.make_async_remote_copy(
                src_ref=y.at[pl.ds(d * L + c * per, per), rows],
                dst_ref=z.at[pl.ds(c * per, per), me, rows],
                send_sem=send1,
                recv_sem=recv1.at[c],
                device_id={"row": d},
                device_id_type=MESH,
            ).start()
            return inner

        lax.fori_loop(1, n, send_to, 0)

    first = (mh[0], ml[0])
    cols = 2 if group % 2 == 0 else 1
    for g in range(G):
        rows = pl.ds(g * group, group)
        pltpu.make_async_copy(x_hbm.at[:, rows], x.at[:, rows], x_sem.at[g]).wait()

        def sweep(s, carry, g=g):
            r = g * group + s * cols
            k = split(react(load_columns(x, r, cols, 0, n * L), rate, level))
            store_columns(y, r, cols, dot3(first, k))
            return carry

        loop_columns(group // cols, x, sweep)
        if g == 0:
            pl.semaphore_wait(barrier, n)
        send_rows(0, rows)

    def own_copy(c):
        return pltpu.make_async_copy(
            y.at[pl.ds(me * L + c * per, per)], z.at[pl.ds(c * per, per), me], own1.at[c]
        )

    def send_chunk(c, carry):
        send_rows(c, pl.ds(0, R))
        own_copy(c).start()
        return carry

    own_copy(0).start()
    lax.fori_loop(1, C, send_chunk, 0)

    depths = orientations(fold(p_depth[...], e_depth[...], True))
    keep(2, flags[0, 2], *depths)
    keep(3, flags[1, 2], *depths)

    half = n * R // 2
    mine = pl.ds(pl.multiple_of(q * half, half), half)
    theirs = pl.ds(pl.multiple_of((1 - q) * half, half), half)
    lanes_mine = pl.ds(pl.multiple_of(q * LANES, LANES), LANES)
    lanes_theirs = pl.ds(pl.multiple_of((1 - q) * LANES, LANES), LANES)
    peer = {"col": 1 - q}

    def back(c):
        return f.at[pl.ds(c * (n * per) + me * per, per)]

    def chunk(c, carry):
        at = pl.ds(c * per, per)
        arrived = z.at[at, pl.ds(0, n - 1)]
        pltpu.make_async_copy(arrived, arrived, recv1.at[c]).wait()
        own_copy(c).wait()

        line = tuple(jnp.concatenate([m[1, mine, :], m[1, theirs, :]], axis=0) for m in (mh, ml))
        for s in range(0, per, pair):
            i = c * per + s
            k = jnp.concatenate([z[i + e].reshape(n * R, LANES) for e in range(pair)], axis=1)
            out = dot3(line, split(react(k, rate, level)))
            for e in range(pair):
                part = out[:, e * LANES : (e + 1) * LANES]
                v[i + e, :, lanes_mine] = part[:half]
                w[i + e] = part[half:]
        to_peer = pltpu.make_async_remote_copy(
            src_ref=w.at[at],
            dst_ref=v.at[at, :, lanes_mine],
            send_sem=a_send.at[c],
            recv_sem=a_recv.at[c],
            device_id=peer,
            device_id_type=MESH,
        )
        to_peer.start()
        to_peer.wait()

        k = v[at].reshape(per * half, 2 * LANES)
        k = dot3(split(react(k, rate, level)), (mh[2], ml[2]))
        depth = tuple(
            jnp.concatenate([m[3, :, lanes_mine], m[3, :, lanes_theirs]], axis=1) for m in (mh, ml)
        )
        k = dot3(split(react(k, rate, level)), depth)
        t[at, mine, :] = k[:, :LANES].reshape(per, half, LANES)
        h[at] = k[:, LANES:].reshape(per, half, LANES)
        to_peer = pltpu.make_async_remote_copy(
            src_ref=h.at[at],
            dst_ref=t.at[at, mine, :],
            send_sem=b_send.at[c],
            recv_sem=b_recv.at[c],
            device_id=peer,
            device_id_type=MESH,
        )
        to_peer.start()
        to_peer.wait()

        line = (mh[4], ml[4])
        for s in range(0, per, pair):
            i = c * per + s
            k = jnp.concatenate([t[i + e] for e in range(pair)], axis=1)
            out = dot3(line, split(react(k, rate, level)))
            for e in range(pair):
                u[i + e] = out[:, e * LANES : (e + 1) * LANES].reshape(n, R, LANES)

        def send_to(j, inner):
            d = lax.rem(me + j, n)
            pltpu.make_async_remote_copy(
                src_ref=u.at[at, d],
                dst_ref=back(c),
                send_sem=send2,
                recv_sem=recv2.at[c],
                device_id={"row": d},
                device_id_type=MESH,
            ).start()
            return inner

        lax.fori_loop(1, n, send_to, 0)
        pltpu.make_async_copy(u.at[at, me], back(c), own2.at[c]).start()
        return carry

    lax.fori_loop(0, C, chunk, 0)

    def wait_back(c, carry):
        arrived = f.at[pl.ds(c * (n * per), (n - 1) * per)]
        pltpu.make_async_copy(arrived, arrived, recv2.at[c]).wait()
        pltpu.make_async_copy(u.at[pl.ds(c * per, per), me], back(c), own2.at[c]).wait()
        return carry

    def terms(matrix, r, start, count):
        hi, lo = split(react(load_columns(f, r, cols, start, count), rate, level))
        k = jnp.concatenate([hi, lo, hi], axis=0)
        return jnp.dot(matrix, k, preferred_element_type=jnp.float32)

    early = (C - 1) * n * per
    if C > 1:
        lax.fori_loop(0, C - 1, wait_back, 0)
        lead = ma[...]

        def begin(s, carry):
            store_columns(x, s * cols, cols, terms(lead, s * cols, 0, early))
            return carry

        loop_columns(R // cols, x, begin)
    wait_back(C - 1, 0)
    rest = mb[...]

    def o_copy(g):
        rows = pl.ds(g * group, group)
        return pltpu.make_async_copy(x.at[:, rows], o_hbm.at[:, rows], o_sem.at[g])

    for g in range(G):

        def finish(s, carry, g=g):
            r = g * group + s * cols
            total = terms(rest, r, early, n * per)
            if C > 1:
                total += load_columns(x, r, cols, 0, n * L)
            store_columns(x, r, cols, total)
            return carry

        loop_columns(group // cols, x, finish)
        o_copy(g).start()

    away = y.at[pl.ds(0, (n - 1) * L)]
    pltpu.make_async_copy(away, away, send1).wait()
    pltpu.make_async_copy(away, away, send2).wait()
    for g in range(G):
        o_copy(g).wait()


def on_device(
    n,
    concentration,
    species,
    reaction_rates,
    levels,
    sweep_flags,
    explicit_line,
    inverse_line,
    explicit_depth,
    inverse_depth,
):
    lines, R, lanes = concentration.shape
    L = lines // n
    C = max(1, L // 4)
    G = max(1, R // 8)
    per = L // C
    half = n * R // 2
    f32, bf16 = jnp.float32, jnp.bfloat16

    c, source, e = np.meshgrid(np.arange(C), np.arange(n), np.arange(per), indexing="ij")
    held = (source * L + c * per + e).reshape(-1)
    early = (C - 1) * n * per
    picks = []
    for part in (held[:early], held[early:]):
        pick = np.zeros((lines, len(part)), np.float32)
        pick[part, np.arange(len(part))] = 1
        none = np.zeros_like(pick)
        picks.append(
            np.stack([np.concatenate(m, 1) for m in ((pick, pick, none), (none, none, pick))])
        )
    if C == 1:
        picks[0] = picks[1]
    pick_a, pick_b = (jnp.asarray(p.astype(bf16)) for p in picks)

    any_spec = pl.BlockSpec(memory_space=pl.ANY)
    smem = pl.BlockSpec(memory_space=pltpu.SMEM)
    vmem = pl.BlockSpec(memory_space=pltpu.VMEM)
    dma = pltpu.SemaphoreType.DMA
    return pl.pallas_call(
        functools.partial(kernel, n, L, R, C, G),
        out_shape=jax.ShapeDtypeStruct(concentration.shape, f32),
        in_specs=[smem] * 4 + [vmem] * 6 + [any_spec],
        out_specs=any_spec,
        scratch_shapes=[
            pltpu.VMEM((lines, R, lanes), f32),
            pltpu.VMEM((lines, R, lanes), f32),
            pltpu.VMEM((L, n, R, lanes), f32),
            pltpu.VMEM((L, half, lanes), f32),
            pltpu.VMEM((L, half, 2 * lanes), f32),
            pltpu.VMEM((L, half, lanes), f32),
            pltpu.VMEM((L, 2 * half, lanes), f32),
            pltpu.VMEM((L, n, R, lanes), f32),
            pltpu.VMEM((lines, R, lanes), f32),
            pltpu.VMEM((5, lines, lines), bf16),
            pltpu.VMEM((5, lines, lines), bf16),
            pltpu.VMEM((lines, pick_a.shape[2]), bf16),
            pltpu.VMEM((lines, pick_b.shape[2]), bf16),
            dma((G,)),
            dma((C,)),
            dma((C,)),
            dma,
            dma((C,)),
            dma,
            dma((C,)),
            dma((C,)),
            dma((C,)),
            dma((C,)),
            dma((C,)),
            dma((G,)),
        ],
        compiler_params=pltpu.CompilerParams(
            collective_id=0, has_side_effects=True, vmem_limit_bytes=58 << 20
        ),
    )(
        species, reaction_rates, levels, sweep_flags,
        explicit_line, inverse_line, explicit_depth, inverse_depth,
        pick_a, pick_b, concentration,
    )


def solution(mesh):
    in_specs = (P("groups", "row", "col"), P("groups"), P(), P(), P(), P(), P(), P(), P())
    out_specs = P("groups", "row", "col")
    return jax.shard_map(
        functools.partial(on_device, mesh.shape["row"]),
        mesh=mesh, in_specs=in_specs, out_specs=out_specs, check_vma=False,
    )
```

time: 219 us -> 205 us (0.936)
  local copies, waits for them, and re-layouts: 10.9 us -> 4.64 us
  other arithmetic: 3.39 us -> 0 us
    another operation x2 -> x0, local copies, waits for them, and re-layouts: 3.85 us -> none  [the longest x1 3.83 us: on_device(): flags = jnp.stack([sweep_flags[s, d] for s, d in order])]
    pallas_call x2 -> x1, Pallas kernels: 201 us -> 199 us  [on_device(): pl.pallas_call(functools.partial(kernel, n, L, R, C, G), out_shape=jax.Sh...]
    unnamed x15 -> x1, local copies, waits for them, and re-layouts: 3.37 us -> 4.64 us
where the time goes in v1:
time: 205 us
  Pallas kernels  199 us (97%)
  local copies, waits for them, and re-layouts  4.64 us (2%)
    pallas_call x1, Pallas kernels, on_device(): pl.pallas_call(functools.partial(kernel, n, L, R, C, G), out_shape=jax.Sh...  199 us
    unnamed x1, local copies, waits for them, and re-layouts  4.64 us

profile of v1, /device:TPU:10, one launch (start us, length us, event | category | flops | bytes accessed | tf_op | source)
XLA Modules:
  0.0 204.6 jit_solution(1793506167999464958)
XLA Ops:
  0.7 199.3 %shard_map.109 = f32[256,32,128]{2,1,0:T(8,128)} custom-call(s32[1]{0:T(128)S(6)} %copy.13.species, f32[64]{0:T(128)} %rates.1, f32[64]{0:T(128)} %levels.1, s32[2,3]{1,0:T(2,128)} %flags.1, f32[256,256]{1,0:T(8,128)} %e_line.1, f32[256,256]{1,0:T(8,128)} %p_line.1, f32[256,256]{1,0:T(8,128)} %e_depth.1, f32[256,256]{1,0:T(8,128)} %p_depth.1, ...), custom_call_target="tpu_custom_call" | custom-call | tf_op jit(solution)/shard_map/pallas_call | solution.py:358
  199.9 4.6 %copy.14 = f32[256,32,128]{2,1,0:T(8,128)} copy(f32[256,32,128]{2,1,0:T(8,128)} %shard_map.109) | data formatting | bytes 8388608

commit v2 on v1

--- a/solution.py
+++ b/solution.py
@@ -91,10 +91,10 @@
 
 def kernel(
     n, L, R, C, G,
-    species, rates, levels, flags, e_line, p_line, e_depth, p_depth, pick_a, pick_b,
-    x_hbm, o_hbm,
-    x, y, z, w, v, h, t, u, f, mh, ml, ma, mb,
-    x_sem, own1, own2, send1, recv1, send2, recv2, a_send, a_recv, b_send, b_recv, o_sem,
+    species, rates, levels, flags, e_line, p_line, late_0, late_1, late_2, late_3,
+    x_hbm, o_hbm, last, mb,
+    x, y, z, w, v, h, t, u, f, mh, ml, ma, e_depth, p_depth, pick_a, pick_b,
+    x_sem, own1, own2, send1, recv1, send2, recv2, a_send, a_recv, b_send, b_recv, o_sem, late_sem,
 ):
     me = lax.axis_index("row")
     q = lax.axis_index("col")
@@ -106,6 +106,15 @@
         rows = pl.ds(g * group, group)
         pltpu.make_async_copy(x_hbm.at[:, rows], x.at[:, rows], x_sem.at[g]).start()
 
+    late = [
+        pltpu.make_async_copy(source, target, late_sem.at[i])
+        for i, (source, target) in enumerate(
+            zip((late_0, late_1, late_2, late_3), (e_depth, p_depth, pick_a, pick_b))
+        )
+    ]
+    for copy in late:
+        copy.start()
+
     barrier = pltpu.get_barrier_semaphore()
 
     def greet(j, carry):
@@ -125,18 +134,6 @@
 
     lines = orientations(fold(p_line[...], e_line[...], False))
     keep(0, flags[0, 0], *lines)
-    keep(1, flags[0, 1], *lines)
-    keep(4, flags[1, 1], *lines)
-    final = choose(flags[1, 0], *lines)
-    if C > 1:
-        ma[...] = (
-            jnp.dot(final[0], pick_a[0], preferred_element_type=jnp.float32)
-            + jnp.dot(final[1], pick_a[1], preferred_element_type=jnp.float32)
-        ).astype(jnp.bfloat16)
-    mb[...] = (
-        jnp.dot(final[0], pick_b[0], preferred_element_type=jnp.float32)
-        + jnp.dot(final[1], pick_b[1], preferred_element_type=jnp.float32)
-    ).astype(jnp.bfloat16)
 
     def send_rows(c, rows):
         def send_to(j, inner):
@@ -168,7 +165,9 @@
         loop_columns(group // cols, x, sweep)
         if g == 0:
             pl.semaphore_wait(barrier, n)
-        send_rows(0, rows)
+            send_rows(0, rows)
+    if G > 1:
+        send_rows(0, pl.ds(group, R - group))
 
     def own_copy(c):
         return pltpu.make_async_copy(
@@ -183,6 +182,19 @@
     own_copy(0).start()
     lax.fori_loop(1, C, send_chunk, 0)
 
+    for copy in late:
+        copy.wait()
+    keep(1, flags[0, 1], *lines)
+    keep(4, flags[1, 1], *lines)
+    final = choose(flags[1, 0], *lines)
+    ma[...] = (
+        jnp.dot(final[0], pick_a[0], preferred_element_type=jnp.float32)
+        + jnp.dot(final[1], pick_a[1], preferred_element_type=jnp.float32)
+    ).astype(jnp.bfloat16)
+    mb[...] = (
+        jnp.dot(final[0], pick_b[0], preferred_element_type=jnp.float32)
+        + jnp.dot(final[1], pick_b[1], preferred_element_type=jnp.float32)
+    ).astype(jnp.bfloat16)
     depths = orientations(fold(p_depth[...], e_depth[...], True))
     keep(2, flags[0, 2], *depths)
     keep(3, flags[1, 2], *depths)
@@ -196,6 +208,8 @@
 
     def back(c):
         return f.at[pl.ds(c * (n * per) + me * per, per)]
+
+    back_last = last.at[pl.ds(me * per, per)]
 
     def chunk(c, carry):
         at = pl.ds(c * per, per)
@@ -250,20 +264,30 @@
             for e in range(pair):
                 u[i + e] = out[:, e * LANES : (e + 1) * LANES].reshape(n, R, LANES)
 
-        def send_to(j, inner):
-            d = lax.rem(me + j, n)
-            pltpu.make_async_remote_copy(
-                src_ref=u.at[at, d],
-                dst_ref=back(c),
-                send_sem=send2,
-                recv_sem=recv2.at[c],
-                device_id={"row": d},
-                device_id_type=MESH,
-            ).start()
-            return inner
-
-        lax.fori_loop(1, n, send_to, 0)
-        pltpu.make_async_copy(u.at[at, me], back(c), own2.at[c]).start()
+        def send_back(target):
+            def send_to(j, inner):
+                d = lax.rem(me + j, n)
+                pltpu.make_async_remote_copy(
+                    src_ref=u.at[at, d],
+                    dst_ref=target,
+                    send_sem=send2,
+                    recv_sem=recv2.at[c],
+                    device_id={"row": d},
+                    device_id_type=MESH,
+                ).start()
+                return inner
+
+            lax.fori_loop(1, n, send_to, 0)
+            pltpu.make_async_copy(u.at[at, me], target, own2.at[c]).start()
+
+        @pl.when(c < C - 1)
+        def _():
+            send_back(back(c))
+
+        @pl.when(c == C - 1)
+        def _():
+            send_back(back_last)
+
         return carry
 
     lax.fori_loop(0, C, chunk, 0)
@@ -274,23 +298,8 @@
         pltpu.make_async_copy(u.at[pl.ds(c * per, per), me], back(c), own2.at[c]).wait()
         return carry
 
-    def terms(matrix, r, start, count):
-        hi, lo = split(react(load_columns(f, r, cols, start, count), rate, level))
-        k = jnp.concatenate([hi, lo, hi], axis=0)
-        return jnp.dot(matrix, k, preferred_element_type=jnp.float32)
-
-    early = (C - 1) * n * per
-    if C > 1:
-        lax.fori_loop(0, C - 1, wait_back, 0)
-        lead = ma[...]
-
-        def begin(s, carry):
-            store_columns(x, s * cols, cols, terms(lead, s * cols, 0, early))
-            return carry
-
-        loop_columns(R // cols, x, begin)
-    wait_back(C - 1, 0)
-    rest = mb[...]
+    lax.fori_loop(0, C - 1, wait_back, 0)
+    lead = ma[...]
 
     def o_copy(g):
         rows = pl.ds(g * group, group)
@@ -298,22 +307,41 @@
 
     for g in range(G):
 
-        def finish(s, carry, g=g):
+        def begin(s, carry, g=g):
             r = g * group + s * cols
-            total = terms(rest, r, early, n * per)
-            if C > 1:
-                total += load_columns(x, r, cols, 0, n * L)
-            store_columns(x, r, cols, total)
+            store_columns(x, r, cols, terms(lead, f, r, cols, rate, level))
             return carry
 
-        loop_columns(group // cols, x, finish)
+        loop_columns(group // cols, x, begin)
         o_copy(g).start()
+    for g in range(G):
+        o_copy(g).wait()
 
     away = y.at[pl.ds(0, (n - 1) * L)]
     pltpu.make_async_copy(away, away, send1).wait()
     pltpu.make_async_copy(away, away, send2).wait()
-    for g in range(G):
-        o_copy(g).wait()
+    arrived = last.at[pl.ds(0, (n - 1) * per)]
+    pltpu.make_async_copy(arrived, arrived, recv2.at[C - 1]).wait()
+    pltpu.make_async_copy(u.at[pl.ds((C - 1) * per, per), me], back_last, own2.at[C - 1]).wait()
+
+
+def terms(matrix, ref, r, cols, rate, level):
+    hi, lo = split(react(load_columns(ref, r, cols, 0, ref.shape[0]), rate, level))
+    k = jnp.concatenate([hi, lo, hi], axis=0)
+    return jnp.dot(matrix, k, preferred_element_type=jnp.float32)
+
+
+def last_kernel(species, rates, levels, matrix_ref, last_ref, sum_ref, o_ref):
+    kind = species[0]
+    rate, level = rates[kind], levels[kind]
+    lines, R, lanes = o_ref.shape
+    cols = 2 if R % 2 == 0 else 1
+    matrix = matrix_ref[...]
+
+    for s in range(R // cols):
+        total = load_columns(sum_ref, s * cols, cols, 0, lines)
+        total += terms(matrix, last_ref, s * cols, cols, rate, level)
+        store_columns(o_ref, s * cols, cols, total)
 
 
 def on_device(
@@ -330,7 +358,7 @@
 ):
     lines, R, lanes = concentration.shape
     L = lines // n
-    C = max(1, L // 4)
+    C = max(2, L // 8)
     G = max(1, R // 8)
     per = L // C
     half = n * R // 2
@@ -347,19 +375,22 @@
         picks.append(
             np.stack([np.concatenate(m, 1) for m in ((pick, pick, none), (none, none, pick))])
         )
-    if C == 1:
-        picks[0] = picks[1]
     pick_a, pick_b = (jnp.asarray(p.astype(bf16)) for p in picks)
 
     any_spec = pl.BlockSpec(memory_space=pl.ANY)
     smem = pl.BlockSpec(memory_space=pltpu.SMEM)
     vmem = pl.BlockSpec(memory_space=pltpu.VMEM)
     dma = pltpu.SemaphoreType.DMA
-    return pl.pallas_call(
+    whole = jax.ShapeDtypeStruct(concentration.shape, f32)
+    partial_sum, last, matrix = pl.pallas_call(
         functools.partial(kernel, n, L, R, C, G),
-        out_shape=jax.ShapeDtypeStruct(concentration.shape, f32),
-        in_specs=[smem] * 4 + [vmem] * 6 + [any_spec],
-        out_specs=any_spec,
+        out_shape=(
+            whole,
+            jax.ShapeDtypeStruct((n * per, R, lanes), f32),
+            jax.ShapeDtypeStruct((lines, pick_b.shape[2]), bf16),
+        ),
+        in_specs=[smem] * 4 + [vmem] * 2 + [any_spec] * 5,
+        out_specs=(any_spec, any_spec, vmem),
         scratch_shapes=[
             pltpu.VMEM((lines, R, lanes), f32),
             pltpu.VMEM((lines, R, lanes), f32),
@@ -369,11 +400,14 @@
             pltpu.VMEM((L, half, lanes), f32),
             pltpu.VMEM((L, 2 * half, lanes), f32),
             pltpu.VMEM((L, n, R, lanes), f32),
-            pltpu.VMEM((lines, R, lanes), f32),
+            pltpu.VMEM((early, R, lanes), f32),
             pltpu.VMEM((5, lines, lines), bf16),
             pltpu.VMEM((5, lines, lines), bf16),
             pltpu.VMEM((lines, pick_a.shape[2]), bf16),
-            pltpu.VMEM((lines, pick_b.shape[2]), bf16),
+            pltpu.VMEM(explicit_depth.shape, f32),
+            pltpu.VMEM(inverse_depth.shape, f32),
+            pltpu.VMEM(pick_a.shape, bf16),
+            pltpu.VMEM(pick_b.shape, bf16),
             dma((G,)),
             dma((C,)),
             dma((C,)),
@@ -386,6 +420,7 @@
             dma((C,)),
             dma((C,)),
             dma((G,)),
+            dma((4,)),
         ],
         compiler_params=pltpu.CompilerParams(
             collective_id=0, has_side_effects=True, vmem_limit_bytes=58 << 20
@@ -396,6 +431,23 @@
         pick_a, pick_b, concentration,
     )
 
+    rows = R // G
+    return pl.pallas_call(
+        last_kernel,
+        grid=(G,),
+        out_shape=whole,
+        in_specs=[
+            smem,
+            smem,
+            smem,
+            pl.BlockSpec(matrix.shape, lambda g: (0, 0)),
+            pl.BlockSpec((n * per, rows, lanes), lambda g: (0, g, 0)),
+            pl.BlockSpec((lines, rows, lanes), lambda g: (0, g, 0)),
+        ],
+        out_specs=pl.BlockSpec((lines, rows, lanes), lambda g: (0, g, 0)),
+        compiler_params=pltpu.CompilerParams(vmem_limit_bytes=58 << 20),
+    )(species, reaction_rates, levels, matrix, last, partial_sum)
+
 
 def solution(mesh):
     in_specs = (P("groups", "row", "col"), P("groups"), P(), P(), P(), P(), P(), P(), P())

time: 205 us -> 196 us (0.956)
  local copies, waits for them, and re-layouts: 4.64 us -> 0 us
  Pallas kernels: 199 us -> 195 us
    unnamed x1 -> x0, local copies, waits for them, and re-layouts: 4.64 us -> none
    pallas_call x1 -> x2, Pallas kernels: 199 us -> 195 us  [the longest x1 189 us: on_device(): pl.pallas_call(functools.partial(kernel, n, L, R, C, G), out_shape=(whole...]
where the time goes in v2:
time: 196 us
  Pallas kernels  195 us (99%)
    pallas_call x1, Pallas kernels, on_device(): pl.pallas_call(functools.partial(kernel, n, L, R, C, G), out_shape=(whole...  189 us
    pallas_call x1, Pallas kernels, on_device(): pl.pallas_call(last_kernel, grid=(G,), out_shape=whole, in_specs=[smem, s...  5.9 us

profile of v2, /device:TPU:10, one launch (start us, length us, event | category | flops | bytes accessed | tf_op | source)
XLA Modules:
  0.0 195.9 jit_solution(13690613934651932930)
XLA Ops:
  0.7 189.3 %shard_map.109 = (f32[256,32,128]{2,1,0:T(8,128)}, f32[64,32,128]{2,1,0:T(8,128)}, bf16[256,192]{1,0:T(8,128)(2,1)}) custom-call(s32[1]{0:T(128)S(6)} %copy.12.species, f32[64]{0:T(128)} %rates.3, f32[64]{0:T(128)} %levels.3, s32[2,3]{1,0:T(2,128)} %flags.1, f32[256,256]{1,0:T(8,128)} %e_line.1, f32[256,256]{1,0:T(8,128)} %p_line.1, f32[256,256]{1,0:T(8,128)} %late_0.1, ...), custom_call_target="tpu_custom_call" | custom-call | tf_op jit(solution)/shard_map/pallas_call | solution.py:385
  190.0 5.9 %shard_map.110 = f32[256,32,128]{2,1,0:T(8,128)} custom-call(s32[1]{0:T(128)S(6)} %copy.12.species, f32[64]{0:T(128)} %rates.3, f32[64]{0:T(128)} %levels.3, bf16[256,192]{1,0:T(8,128)(2,1)} %get-tuple-element.8.matrix_ref, f32[64,32,128]{2,1,0:T(8,128)} %get-tuple-element.9.last_ref, f32[256,32,128]{2,1,0:T(8,128)} %get-tuple-element.10.sum_ref), custom_call_target="tpu_custom_call" | custom-call | tf_op jit(solution)/shard_map/pallas_call | solution.py:435

commit v3 on v2

--- a/solution.py
+++ b/solution.py
@@ -358,7 +358,7 @@
 ):
     lines, R, lanes = concentration.shape
     L = lines // n
-    C = max(2, L // 8)
+    C = max(2, L // 16)
     G = max(1, R // 8)
     per = L // C
     half = n * R // 2

time: 196 us -> 195 us (level)
  no operation moved by 1% of the time
where the time goes in v3:
time: 195 us
  Pallas kernels  194 us (99%)
    pallas_call x1, Pallas kernels, on_device(): pl.pallas_call(functools.partial(kernel, n, L, R, C, G), out_shape=(whole...  188 us
    pallas_call x1, Pallas kernels, on_device(): pl.pallas_call(last_kernel, grid=(G,), out_shape=whole, in_specs=[smem, s...  6.41 us

profile of v3, /device:TPU:10, one launch (start us, length us, event | category | flops | bytes accessed | tf_op | source)
XLA Modules:
  0.0 194.8 jit_solution(8404961415504251806)
XLA Ops:
  0.7 187.7 %shard_map.109 = (f32[256,32,128]{2,1,0:T(8,128)}, f32[128,32,128]{2,1,0:T(8,128)}, bf16[256,384]{1,0:T(8,128)(2,1)}) custom-call(s32[1]{0:T(128)S(6)} %copy.12.species, f32[64]{0:T(128)} %rates.3, f32[64]{0:T(128)} %levels.3, s32[2,3]{1,0:T(2,128)} %flags.1, f32[256,256]{1,0:T(8,128)} %e_line.1, f32[256,256]{1,0:T(8,128)} %p_line.1, f32[256,256]{1,0:T(8,128)} %late_0.1, ...), custom_call_target="tpu_custom_call" | custom-call | tf_op jit(solution)/shard_map/pallas_call | solution.py:385
  188.3 6.4 %shard_map.110 = f32[256,32,128]{2,1,0:T(8,128)} custom-call(s32[1]{0:T(128)S(6)} %copy.12.species, f32[64]{0:T(128)} %rates.3, f32[64]{0:T(128)} %levels.3, bf16[256,384]{1,0:T(8,128)(2,1)} %get-tuple-element.8.matrix_ref, f32[128,32,128]{2,1,0:T(8,128)} %get-tuple-element.9.last_ref, f32[256,32,128]{2,1,0:T(8,128)} %get-tuple-element.10.sum_ref), custom_call_target="tpu_custom_call" | custom-call | tf_op jit(solution)/shard_map/pallas_call | solution.py:435
